TPU v7x, 128 devices: a whole 4x4x4 slice. The times are simulated.
128 devices in a mesh: ublk: 16 (over x, z), salt: 8 (over y, core).
Axes of the slice: x: 4, y: 4, z: 4, core: 2. Of those that a mesh axis runs over, the one named last changes fastest.
Arguments:
- user_factors: bfloat16 [16, 8192, 256], P('ublk', 'salt')
- tile_users: int32 [16, 8, 4096], P('ublk', 'salt'), may hold values from 0 to 8191
- tile_items: int32 [16, 8, 4096], P('ublk', 'salt'), may hold values from 0 to 511
- tile_weight: float32 [16, 8, 4096], P('ublk', 'salt'), may hold values from 0.5 to 8
- live_count: int32 [16, 8], P('ublk', 'salt'), may hold values from 2048 to 4096, as said below
Outputs:
- item_factors: float32 [8, 512, 256], P('salt', 'ublk')
- residual: float32 [8, 512, 256], P('salt', 'ublk')
Inputs may be any that keep to these rules, and one draw needn't show every extreme that they name: Every entry of live_count is at least 2048 and at most 4096; some tile is full.
All inputs are finite; a program needn't handle non-finite values.
Results may differ from a plain program's by a relative error of at most 0.0022.
Values may be sent and summed in bfloat16 or wider, within the bound.
A program may use at most 64 MiB of HBM per device.

v0:
```python
import jax
import jax.numpy as jnp
from jax import lax
from jax.sharding import PartitionSpec as P

ITERS = 8
ITEM_DEV = 32
REG = 1.0
EPS = 1e-06


def conjugate(rhs, image_of):
    solution = jnp.zeros_like(rhs)
    resid = rhs
    direction = rhs
    norm_now = jnp.sum(resid * resid, axis=1)
    for step in range(ITERS):
        image = image_of(direction)
        alpha = norm_now / (jnp.sum(direction * image, axis=1) + EPS)
        solution = solution + alpha[:, None] * direction
        resid = resid - alpha[:, None] * image
        norm_next = jnp.sum(resid * resid, axis=1)
        direction = resid + (norm_next / (norm_now + EPS))[:, None] * direction
        norm_now = norm_next
    return (solution, resid)


def body(user_factors, tile_users, tile_items, tile_weight, live_count):
    shard = user_factors[0]
    block = lax.all_gather(shard, "salt", axis=0, tiled=True)
    contract = (((0,), (0,)), ((), ()))
    own_gram = lax.dot_general(shard, shard, contract, preferred_element_type=jnp.float32)
    gram = lax.psum(own_gram, ("ublk", "salt"))
    users = tile_users[0, 0]
    items = tile_items[0, 0]
    raw = tile_weight[0, 0]
    live = jnp.arange(users.shape[0], dtype=jnp.int32) < live_count[0, 0]
    weight = jnp.where(live, raw, jnp.zeros_like(raw))
    confid = jnp.where(live, 1.0 + raw, jnp.zeros_like(raw))
    rows = jnp.take(block, users, axis=0).astype(jnp.float32)
    column_items = ITEM_DEV * lax.axis_size("ublk")
    rhs_terms = jax.ops.segment_sum(confid[:, None] * rows, items, num_segments=column_items)

    def local_terms(whole_dir):
        along = jnp.sum(rows * whole_dir[items], axis=1) * weight
        return jax.ops.segment_sum(along[:, None] * rows, items, num_segments=column_items)

    def finish(summed, direction):
        return summed + jnp.dot(direction, gram, precision=lax.Precision.HIGHEST) + REG * direction

    rhs = lax.psum(rhs_terms, "ublk")

    def image_every(direction):
        summed = lax.psum(local_terms(direction), "ublk")
        return finish(summed, direction)

    solution_all, resid_all = conjugate(rhs, image_every)
    start = lax.axis_index("ublk") * ITEM_DEV
    solution = lax.dynamic_slice_in_dim(solution_all, start, ITEM_DEV, 0)
    resid = lax.dynamic_slice_in_dim(resid_all, start, ITEM_DEV, 0)
    return (solution[None], resid[None])


def solution(mesh):
    return jax.shard_map(
        body,
        mesh=mesh,
        in_specs=(
            P("ublk", "salt", None),
            P("ublk", "salt", None),
            P("ublk", "salt", None),
            P("ublk", "salt", None),
            P("ublk", "salt"),
        ),
        out_specs=(P("salt", "ublk", None), P("salt", "ublk", None)),
        check_vma=False,
    )
```

profile of v0, /device:TPU:0, one launch (start us, length us, event | category | flops | bytes accessed | tf_op | source)
XLA Modules:
  0.0 1352.9 jit_solution(7503660293953594438)
XLA Ops:
  10.8 33.5 %all-gather.3.cloned.1.call-done = bf16[1,8192,256]{2,1,0:T(8,128)(2,1)} async-done(((bf16[1,1024,256]{2,1,0:T(8,128)(2,1)}), bf16[1,8192,256]{2,1,0:T(8,128)(2,1)}) %all-gather.3.cloned.1.call-update) | async-done | bytes 4194320 | tf_op jit(solution)/shard_map/all_gather | solution.py:30
  60.1 26.1 %scatter_custom_fusion = f32[512,256]{1,0:T(8,128)} fusion(s32[4096]{0:T(1024)S(1)} %bitcast.56, f32[4096]{0:T(1024)S(1)} %add_select_fusion, f32[]{:T(128)} %constant.11.clone.1, bf16[4096,256]{1,0:T(8,128)(2,1)S(1)} %gather_fusion, pred[4096]{0:T(1024)(128)(4,1)S(1)} %compare_and_fusion), kind=kCustom, calls=%fused_computation.35 | custom fusion | flops 4194304 | bytes 2641924 | tf_op jit(solution)/shard_map/scatter-add | solution.py:42
  87.4 84.7 %all-reduce.11.cloned.1.call-done = f32[512,256]{1,0:T(8,128)} async-done(((f32[512,256]{1,0:T(8,128)}), f32[512,256]{1,0:T(8,128)}) %all-reduce.11.cloned.1.call-update) | async-done | bytes 524304 | tf_op jit(solution)/shard_map/psum | solution.py:51
  172.1 17.1 %gather_fusion.1 = f32[4096,256]{1,0:T(8,128)} fusion(f32[512,256]{1,0:T(8,128)} %all-reduce.11.cloned.1.call-done, s32[4096]{0:T(1024)S(1)} %broadcast_clamp_fusion), kind=kCustom, calls=%fused_computation.1 | custom fusion | bytes 8404992 | tf_op jit(solution)/shard_map/gather | solution.py:45
  192.2 26.1 %scatter_custom_fusion.1 = f32[512,256]{1,0:T(8,128)} fusion(s32[4096]{0:T(1024)S(1)} %bitcast.57, f32[4096]{0:T(1024)S(1)} %fusion.60, f32[]{:T(128)} %constant.11.clone.1, bf16[4096,256]{1,0:T(8,128)(2,1)S(1)} %gather_fusion, pred[4096]{0:T(1024)(128)(4,1)S(1)} %compare_and_fusion), kind=kCustom, calls=%fused_computation.37 | custom fusion | flops 4194304 | bytes 2641924 | tf_op jit(solution)/shard_map/scatter-add | solution.py:46
  218.7 100.7 %all-reduce.15.cloned.1.call-done = f32[256,256]{1,0:T(8,128)} async-done(((f32[256,256]{1,0:T(8,128)}), f32[256,256]{1,0:T(8,128)}) %all-reduce.15.cloned.1.call-update) | async-done | bytes 262160 | tf_op jit(solution)/shard_map/psum | solution.py:33
  319.4 86.2 %all-reduce.13.cloned.1.call-done = f32[512,256]{1,0:T(8,128)} async-done(((f32[512,256]{1,0:T(8,128)}), f32[512,256]{1,0:T(8,128)}) %all-reduce.13.cloned.1.call-update) | async-done | bytes 524304 | tf_op jit(solution)/shard_map/psum | solution.py:54
  408.4 16.1 %gather_fusion.2 = f32[4096,256]{1,0:T(8,128)} fusion(f32[512,256]{1,0:T(8,128)S(1)} %multiply_add_fusion.7, s32[4096]{0:T(1024)S(1)} %broadcast_clamp_fusion), kind=kCustom, calls=%fused_computation.2 | custom fusion | bytes 8404992 | tf_op jit(solution)/shard_map/gather | solution.py:45
  427.5 26.1 %scatter_custom_fusion.2 = f32[512,256]{1,0:T(8,128)} fusion(s32[4096]{0:T(1024)S(1)} %bitcast.58, f32[4096]{0:T(1024)S(1)} %fusion.59, f32[]{:T(128)} %constant.11.clone.1, bf16[4096,256]{1,0:T(8,128)(2,1)S(1)} %gather_fusion, pred[4096]{0:T(1024)(128)(4,1)S(1)} %compare_and_fusion), kind=kCustom, calls=%fused_computation.39 | custom fusion | flops 4194304 | bytes 2641924 | tf_op jit(solution)/shard_map/scatter-add | solution.py:46
  453.7 85.3 %all-reduce.17.cloned.1.call-done = f32[512,256]{1,0:T(8,128)} async-done(((f32[512,256]{1,0:T(8,128)}), f32[512,256]{1,0:T(8,128)}) %all-reduce.17.cloned.1.call-update) | async-done | bytes 524304 | tf_op jit(solution)/shard_map/psum | solution.py:54
  562.5 26.5 %scatter_custom_fusion.3 = f32[512,256]{1,0:T(8,128)} fusion(s32[4096]{0:T(1024)S(1)} %bitcast.59, f32[4096]{0:T(1024)S(1)} %fusion.58, f32[]{:T(128)} %constant.11.clone.1, bf16[4096,256]{1,0:T(8,128)(2,1)} %copy-done.1, pred[4096]{0:T(1024)(128)(4,1)S(1)} %compare_and_fusion), kind=kCustom, calls=%fused_computation.41 | custom fusion | flops 4194304 | bytes 2641924 | tf_op jit(solution)/shard_map/scatter-add | solution.py:46
  589.6 84.6 %all-reduce.19.cloned.1.call-done = f32[512,256]{1,0:T(8,128)} async-done(((f32[512,256]{1,0:T(8,128)}), f32[512,256]{1,0:T(8,128)}) %all-reduce.19.cloned.1.call-update) | async-done | bytes 524304 | tf_op jit(solution)/shard_map/psum | solution.py:54
  696.4 26.1 %scatter_custom_fusion.4 = f32[512,256]{1,0:T(8,128)} fusion(s32[4096]{0:T(1024)S(1)} %bitcast.60, f32[4096]{0:T(1024)S(1)} %fusion.57, f32[]{:T(128)} %constant.11.clone.1, bf16[4096,256]{1,0:T(8,128)(2,1)S(1)} %copy-done.2, pred[4096]{0:T(1024)(128)(4,1)S(1)} %compare_and_fusion), kind=kCustom, calls=%fused_computation.43 | custom fusion | flops 4194304 | bytes 2641924 | tf_op jit(solution)/shard_map/scatter-add | solution.py:46
  722.6 85.2 %all-reduce.21.cloned.1.call-done = f32[512,256]{1,0:T(8,128)} async-done(((f32[512,256]{1,0:T(8,128)}), f32[512,256]{1,0:T(8,128)}) %all-reduce.21.cloned.1.call-update) | async-done | bytes 524304 | tf_op jit(solution)/shard_map/psum | solution.py:54
  810.7 16.1 %gather_fusion.5 = f32[4096,256]{1,0:T(8,128)} fusion(f32[512,256]{1,0:T(8,128)S(1)} %multiply_add_fusion.3, s32[4096]{0:T(1024)S(1)} %broadcast_clamp_fusion), kind=kCustom, calls=%fused_computation.5 | custom fusion | bytes 8404992 | tf_op jit(solution)/shard_map/gather | solution.py:45
  829.7 26.1 %scatter_custom_fusion.5 = f32[512,256]{1,0:T(8,128)} fusion(s32[4096]{0:T(1024)S(1)} %bitcast.61, f32[4096]{0:T(1024)S(1)} %fusion.56, f32[]{:T(128)} %constant.11.clone.1, bf16[4096,256]{1,0:T(8,128)(2,1)S(1)} %copy-done.2, pred[4096]{0:T(1024)(128)(4,1)S(1)} %compare_and_fusion), kind=kCustom, calls=%fused_computation.45 | custom fusion | flops 4194304 | bytes 2641924 | tf_op jit(solution)/shard_map/scatter-add | solution.py:46
  856.1 85.1 %all-reduce.23.cloned.1.call-done = f32[512,256]{1,0:T(8,128)} async-done(((f32[512,256]{1,0:T(8,128)}), f32[512,256]{1,0:T(8,128)}) %all-reduce.23.cloned.1.call-update) | async-done | bytes 524304 | tf_op jit(solution)/shard_map/psum | solution.py:54
  963.9 26.5 %scatter_custom_fusion.6 = f32[512,256]{1,0:T(8,128)} fusion(s32[4096]{0:T(1024)S(1)} %bitcast.62, f32[4096]{0:T(1024)S(1)} %fusion.55, f32[]{:T(128)} %constant.11.clone.1, bf16[4096,256]{1,0:T(8,128)(2,1)} %copy-done.1, pred[4096]{0:T(1024)(128)(4,1)S(1)} %compare_and_fusion), kind=kCustom, calls=%fused_computation.47 | custom fusion | flops 4194304 | bytes 2641924 | tf_op jit(solution)/shard_map/scatter-add | solution.py:46
  990.5 85.2 %all-reduce.25.cloned.1.call-done = f32[512,256]{1,0:T(8,128)} async-done(((f32[512,256]{1,0:T(8,128)}), f32[512,256]{1,0:T(8,128)}) %all-reduce.25.cloned.1.call-update) | async-done | bytes 524304 | tf_op jit(solution)/shard_map/psum | solution.py:54
  1077.9 16.1 %gather_fusion.7 = f32[4096,256]{1,0:T(8,128)} fusion(f32[512,256]{1,0:T(8,128)S(1)} %multiply_add_fusion.1, s32[4096]{0:T(1024)S(1)} %broadcast_clamp_fusion), kind=kCustom, calls=%fused_computation.7 | custom fusion | bytes 8404992 | tf_op jit(solution)/shard_map/gather | solution.py:45
  1097.5 26.5 %scatter_custom_fusion.7 = f32[512,256]{1,0:T(8,128)} fusion(s32[4096]{0:T(1024)S(1)} %bitcast.63, f32[4096]{0:T(1024)S(1)} %fusion.54, f32[]{:T(128)} %constant.11.clone.1, bf16[4096,256]{1,0:T(8,128)(2,1)} %copy-done.1, pred[4096]{0:T(1024)(128)(4,1)S(1)} %compare_and_fusion), kind=kCustom, calls=%fused_computation.49 | custom fusion | flops 4194304 | bytes 2641924 | tf_op jit(solution)/shard_map/scatter-add | solution.py:46
  1124.3 85.0 %all-reduce.27.cloned.1.call-done = f32[512,256]{1,0:T(8,128)} async-done(((f32[512,256]{1,0:T(8,128)}), f32[512,256]{1,0:T(8,128)}) %all-reduce.27.cloned.1.call-update) | async-done | bytes 524304 | tf_op jit(solution)/shard_map/psum | solution.py:54
  1231.0 26.5 %scatter_custom_fusion.8 = f32[512,256]{1,0:T(8,128)} fusion(s32[4096]{0:T(1024)S(1)} %bitcast.64, f32[4096]{0:T(1024)S(1)} %fusion.53, f32[]{:T(128)} %constant.11.clone.1, bf16[4096,256]{1,0:T(8,128)(2,1)} %copy-done.1, pred[4096]{0:T(1024)(128)(4,1)S(1)} %compare_and_fusion), kind=kCustom, calls=%fused_computation.51 | custom fusion | flops 4194304 | bytes 2641924 | tf_op jit(solution)/shard_map/scatter-add | solution.py:46
  1257.8 85.0 %all-reduce.29.cloned.1.call-done = f32[512,256]{1,0:T(8,128)} async-done(((f32[512,256]{1,0:T(8,128)}), f32[512,256]{1,0:T(8,128)}) %all-reduce.29.cloned.1.call-update) | async-done | bytes 524304 | tf_op jit(solution)/shard_map/psum | solution.py:54
  (115 shorter events, 135.3 us)
Async XLA Ops:
  7.2 37.1 %all-gather.3.cloned.1.call-start = ((), (), s32[]{:S(2)}) async-start(), calls=%async_computation.10 | async-start | bytes 4718592 | tf_op jit(solution)/shard_map/all_gather | solution.py:30
  7.9 164.2 %all-reduce.11.cloned.1.call-start = ((), (), s32[]{:S(2)}) async-start(), calls=%async_computation | async-start | bytes 1048576 | tf_op jit(solution)/shard_map/psum | solution.py:51
  44.3 15.8 %copy-start.10 = (s32[1,1,4096]{2,1,0:T(1,128)S(1)}, s32[1,1,4096]{2,1,0:T(1,128)}, u32[]{:S(2)}) copy-start(s32[1,1,4096]{2,1,0:T(1,128)} %param.7) | copy-start | bytes 49156
  44.3 42.0 %copy-start.9 = (bf16[1,1024,256]{2,1,0:T(8,128)(2,1)S(1)}, bf16[1,1024,256]{2,1,0:T(8,128)(2,1)}, u32[]{:S(2)}) copy-start(bf16[1,1024,256]{2,1,0:T(8,128)(2,1)} %param.5) | copy-start | bytes 1572868
  60.1 367.5 %copy-start.1 = (bf16[4096,256]{1,0:T(8,128)(2,1)}, bf16[4096,256]{1,0:T(8,128)(2,1)S(1)}, u32[]{:S(2)}) copy-start(bf16[4096,256]{1,0:T(8,128)(2,1)S(1)} %gather_fusion) | copy-start | bytes 6291460
  86.2 233.2 %all-reduce.15.cloned.1.call-start = ((), (), s32[]{:S(2)}) async-start(), calls=%async_computation.2 | async-start | bytes 524288 | tf_op jit(solution)/shard_map/psum | solution.py:33
  87.3 318.2 %all-reduce.13.cloned.1.call-start = ((), (), s32[]{:S(2)}) async-start(), calls=%async_computation.1 | async-start | bytes 1048576 | tf_op jit(solution)/shard_map/psum | solution.py:54
  189.2 3.0 copy-start.8
  189.2 216.4 %copy-start = (f32[512,256]{1,0:T(8,128)S(1)}, f32[512,256]{1,0:T(8,128)}, u32[]{:S(2)}) copy-start(f32[512,256]{1,0:T(8,128)} %all-reduce.11.cloned.1.call-done) | copy-start | bytes 1572868
  218.4 320.6 %all-reduce.17.cloned.1.call-start = ((), (), s32[]{:S(2)}) async-start(), calls=%async_computation.3 | async-start | bytes 1048576 | tf_op jit(solution)/shard_map/psum | solution.py:54
  407.4 0.8 copy-start.4
  424.5 114.5 %copy-start.3 = (f32[256,256]{1,0:T(8,128)S(1)}, f32[256,256]{1,0:T(8,128)}, u32[]{:S(2)}) copy-start(f32[256,256]{1,0:T(8,128)} %all-reduce.15.cloned.1.call-done) | copy-start | bytes 786436
  453.6 220.6 %all-reduce.19.cloned.1.call-start = ((), (), s32[]{:S(2)}) async-start(), calls=%async_computation.4 | async-start | bytes 1048576 | tf_op jit(solution)/shard_map/psum | solution.py:54
  589.0 218.8 %all-reduce.21.cloned.1.call-start = ((), (), s32[]{:S(2)}) async-start(), calls=%async_computation.5 | async-start | bytes 1048576 | tf_op jit(solution)/shard_map/psum | solution.py:54
  676.2 1.0 copy-start.6
  677.3 16.1 %copy-start.2 = (bf16[4096,256]{1,0:T(8,128)(2,1)S(1)}, bf16[4096,256]{1,0:T(8,128)(2,1)}, u32[]{:S(2)}) copy-start(bf16[4096,256]{1,0:T(8,128)(2,1)} %copy-done.1) | copy-start | bytes 6291460
  693.3 116.2 %copy-start.7 = (f32[512,256]{1,0:T(8,128)S(1)}, f32[512,256]{1,0:T(8,128)}, u32[]{:S(2)}) copy-start(f32[512,256]{1,0:T(8,128)} %copy-done.6) | copy-start | bytes 1572868
  722.5 218.7 %all-reduce.23.cloned.1.call-start = ((), (), s32[]{:S(2)}) async-start(), calls=%async_computation.6 | async-start | bytes 1048576 | tf_op jit(solution)/shard_map/psum | solution.py:54
  809.8 0.8 copy-start.5
  855.9 219.9 %all-reduce.25.cloned.1.call-start = ((), (), s32[]{:S(2)}) async-start(), calls=%async_computation.7 | async-start | bytes 1048576 | tf_op jit(solution)/shard_map/psum | solution.py:54
  990.5 218.8 %all-reduce.27.cloned.1.call-start = ((), (), s32[]{:S(2)}) async-start(), calls=%async_computation.8 | async-start | bytes 1048576 | tf_op jit(solution)/shard_map/psum | solution.py:54
  1124.0 218.8 %all-reduce.29.cloned.1.call-start = ((), (), s32[]{:S(2)}) async-start(), calls=%async_computation.9 | async-start | bytes 1048576 | tf_op jit(solution)/shard_map/psum | solution.py:54
Sparse Core Ops, SparseCore 0:
  9.7 34.5 all-gather.2
  86.3 85.7 all-reduce.10
  176.8 142.5 all-reduce.14
  322.5 83.0 all-reduce.12
  453.8 85.1 all-reduce.16
  589.2 85.0 all-reduce.18
  722.6 85.1 all-reduce.20
  856.0 85.1 all-reduce.22
  990.6 85.1 all-reduce.24
  1124.1 85.1 all-reduce.26
  1257.6 85.1 all-reduce.28
where the time goes:
time: 1360 us; the launch traced here: 1350 us
  waiting for transfers between devices  901 us (66%)
  other arithmetic  273 us (20%)
  local copies, waits for them, and re-layouts  147 us (11%)
  between operations  15.1 us (1%)
  matrix products  14.8 us (1%)
    psum x8, waiting for transfers between devices, image_every(): summed = lax.psum(local_terms(direction), 'ublk')  682 us
    scatter-add x8, other arithmetic, local_terms(): jax.ops.segment_sum(along[:, None] * rows, items, num_segments=column_items)  210 us
    gather x8, local copies, waits for them, and re-layouts, local_terms(): along = jnp.sum(rows * whole_dir[items], axis=1) * weight  130 us
    psum x1, waiting for transfers between devices, body(): gram = lax.psum(own_gram, ('ublk', 'salt'))  101 us
    psum x1, waiting for transfers between devices, body(): rhs = lax.psum(rhs_terms, 'ublk')  84.7 us
    all_gather x1, waiting for transfers between devices, body(): block = lax.all_gather(shard, 'salt', axis=0, tiled=True)  33.5 us
  transfers between devices with their start and end apart: 11, of which 11 were waited for; matrix products, arithmetic and copies ran while one was open for 4% of the time, Pallas kernels for 0%

commit v1 on v0

--- a/solution.py
+++ b/solution.py
@@ -48,7 +48,9 @@
     def finish(summed, direction):
         return summed + jnp.dot(direction, gram, precision=lax.Precision.HIGHEST) + REG * direction
 
-    rhs = lax.psum(rhs_terms, "ublk")
+    rhs = rhs_terms
+    for hop in (1, 2, 4, 8):
+        rhs = rhs + lax.ppermute(rhs, "ublk", [(dev, dev ^ hop) for dev in range(16)])
 
     def image_every(direction):
         summed = lax.psum(local_terms(direction), "ublk")

time: 1360 us -> 1300 us (0.956)
  waiting for transfers between devices: 901 us -> 833 us
    psum x1 -> x0, waiting for transfers between devices: 84.7 us -> none  [body(): rhs = lax.psum(rhs_terms, 'ublk')]
    ppermute x0 -> x4, waiting for transfers between devices: none -> 43.1 us  [body(): lax.ppermute(rhs, 'ublk', [(dev, dev ^ hop) for dev in range(16)])]
    psum x1, waiting for transfers between devices: 101 us -> 78.1 us  [body(): gram = lax.psum(own_gram, ('ublk', 'salt'))]
  transfers between devices with their start and end apart: 11 -> 14, of which waited for: 11 -> 14; matrix products, arithmetic and copies ran while one was open for 4% -> 4% of each run, Pallas kernels for 0% -> 0%
where the time goes in v1:
time: 1300 us
  waiting for transfers between devices  833 us (64%)
  other arithmetic  272 us (21%)
  local copies, waits for them, and re-layouts  146 us (11%)
  between operations  17 us (1%)
  matrix products  16 us (1%)
    psum x8, waiting for transfers between devices, image_every(): summed = lax.psum(local_terms(direction), 'ublk')  678 us
    scatter-add x8, other arithmetic, local_terms(): jax.ops.segment_sum(along[:, None] * rows, items, num_segments=column_items)  210 us
    gather x8, local copies, waits for them, and re-layouts, local_terms(): along = jnp.sum(rows * whole_dir[items], axis=1) * weight  129 us
    psum x1, waiting for transfers between devices, body(): gram = lax.psum(own_gram, ('ublk', 'salt'))  78.1 us
    ppermute x4, waiting for transfers between devices, body(): lax.ppermute(rhs, 'ublk', [(dev, dev ^ hop) for dev in range(16)])  43.1 us
    all_gather x1, waiting for transfers between devices, body(): block = lax.all_gather(shard, 'salt', axis=0, tiled=True)  33.5 us
  transfers between devices with their start and end apart: 14, of which 14 were waited for; matrix products, arithmetic and copies ran while one was open for 4% of the time, Pallas kernels for 0%

profile of v1, /device:TPU:0, one launch (start us, length us, event | category | flops | bytes accessed | tf_op | source)
XLA Modules:
  0.0 1295.6 jit_solution(15525109093016080871)
XLA Ops:
  11.6 33.5 %all-gather.3.cloned.1.call-done = bf16[1,8192,256]{2,1,0:T(8,128)(2,1)} async-done(((bf16[1,1024,256]{2,1,0:T(8,128)(2,1)}), bf16[1,8192,256]{2,1,0:T(8,128)(2,1)}) %all-gather.3.cloned.1.call-update) | async-done | bytes 4194320 | tf_op jit(solution)/shard_map/all_gather | solution.py:30
  60.9 25.4 %scatter_custom_fusion = f32[512,256]{1,0:T(8,128)S(1)} fusion(s32[4096]{0:T(1024)S(1)} %bitcast.56, f32[4096]{0:T(1024)S(1)} %add_select_fusion, f32[]{:T(128)} %constant.11.clone.1, bf16[4096,256]{1,0:T(8,128)(2,1)S(1)} %gather_fusion, pred[4096]{0:T(1024)(128)(4,1)S(1)} %compare_and_fusion), kind=kCustom, calls=%fused_computation.35 | custom fusion | flops 4194304 | bytes 2641924 | tf_op jit(solution)/shard_map/scatter-add | solution.py:42
  141.6 16.1 %gather_fusion.1 = f32[4096,256]{1,0:T(8,128)} fusion(f32[512,256]{1,0:T(8,128)S(1)} %add.304, s32[4096]{0:T(1024)S(1)} %broadcast_clamp_fusion), kind=kCustom, calls=%fused_computation.1 | custom fusion | bytes 8404992 | tf_op jit(solution)/shard_map/gather | solution.py:45
  160.7 26.1 %scatter_custom_fusion.1 = f32[512,256]{1,0:T(8,128)} fusion(s32[4096]{0:T(1024)S(1)} %bitcast.57, f32[4096]{0:T(1024)S(1)} %fusion.60, f32[]{:T(128)} %constant.11.clone.1, bf16[4096,256]{1,0:T(8,128)(2,1)S(1)} %gather_fusion, pred[4096]{0:T(1024)(128)(4,1)S(1)} %compare_and_fusion), kind=kCustom, calls=%fused_computation.37 | custom fusion | flops 4194304 | bytes 2641924 | tf_op jit(solution)/shard_map/scatter-add | solution.py:46
  187.1 78.1 %all-reduce.12.cloned.1.call-done = f32[256,256]{1,0:T(8,128)} async-done(((f32[256,256]{1,0:T(8,128)}), f32[256,256]{1,0:T(8,128)}) %all-reduce.12.cloned.1.call-update) | async-done | bytes 262160 | tf_op jit(solution)/shard_map/psum | solution.py:33
  265.3 85.7 %all-reduce.10.cloned.1.call-done = f32[512,256]{1,0:T(8,128)} async-done(((f32[512,256]{1,0:T(8,128)}), f32[512,256]{1,0:T(8,128)}) %all-reduce.10.cloned.1.call-update) | async-done | bytes 524304 | tf_op jit(solution)/shard_map/psum | solution.py:56
  353.9 16.1 %gather_fusion.2 = f32[4096,256]{1,0:T(8,128)} fusion(f32[512,256]{1,0:T(8,128)S(1)} %multiply_add_fusion.7, s32[4096]{0:T(1024)S(1)} %broadcast_clamp_fusion), kind=kCustom, calls=%fused_computation.2 | custom fusion | bytes 8404992 | tf_op jit(solution)/shard_map/gather | solution.py:45
  372.9 26.1 %scatter_custom_fusion.2 = f32[512,256]{1,0:T(8,128)} fusion(s32[4096]{0:T(1024)S(1)} %bitcast.58, f32[4096]{0:T(1024)S(1)} %fusion.59, f32[]{:T(128)} %constant.11.clone.1, bf16[4096,256]{1,0:T(8,128)(2,1)S(1)} %gather_fusion, pred[4096]{0:T(1024)(128)(4,1)S(1)} %compare_and_fusion), kind=kCustom, calls=%fused_computation.39 | custom fusion | flops 4194304 | bytes 2641924 | tf_op jit(solution)/shard_map/scatter-add | solution.py:46
  399.1 84.7 %all-reduce.14.cloned.1.call-done = f32[512,256]{1,0:T(8,128)} async-done(((f32[512,256]{1,0:T(8,128)}), f32[512,256]{1,0:T(8,128)}) %all-reduce.14.cloned.1.call-update) | async-done | bytes 524304 | tf_op jit(solution)/shard_map/psum | solution.py:56
  487.8 16.1 %gather_fusion.3 = f32[4096,256]{1,0:T(8,128)} fusion(f32[512,256]{1,0:T(8,128)S(1)} %multiply_add_fusion.5, s32[4096]{0:T(1024)S(1)} %broadcast_clamp_fusion), kind=kCustom, calls=%fused_computation.3 | custom fusion | bytes 8404992 | tf_op jit(solution)/shard_map/gather | solution.py:45
  507.4 26.5 %scatter_custom_fusion.3 = f32[512,256]{1,0:T(8,128)} fusion(s32[4096]{0:T(1024)S(1)} %bitcast.59, f32[4096]{0:T(1024)S(1)} %fusion.58, f32[]{:T(128)} %constant.11.clone.1, bf16[4096,256]{1,0:T(8,128)(2,1)} %copy-done, pred[4096]{0:T(1024)(128)(4,1)S(1)} %compare_and_fusion), kind=kCustom, calls=%fused_computation.41 | custom fusion | flops 4194304 | bytes 2641924 | tf_op jit(solution)/shard_map/scatter-add | solution.py:46
  534.5 84.2 %all-reduce.16.cloned.1.call-done = f32[512,256]{1,0:T(8,128)} async-done(((f32[512,256]{1,0:T(8,128)}), f32[512,256]{1,0:T(8,128)}) %all-reduce.16.cloned.1.call-update) | async-done | bytes 524304 | tf_op jit(solution)/shard_map/psum | solution.py:56
  640.8 26.1 %scatter_custom_fusion.4 = f32[512,256]{1,0:T(8,128)} fusion(s32[4096]{0:T(1024)S(1)} %bitcast.60, f32[4096]{0:T(1024)S(1)} %fusion.57, f32[]{:T(128)} %constant.11.clone.1, bf16[4096,256]{1,0:T(8,128)(2,1)S(1)} %copy-done.1, pred[4096]{0:T(1024)(128)(4,1)S(1)} %compare_and_fusion), kind=kCustom, calls=%fused_computation.43 | custom fusion | flops 4194304 | bytes 2641924 | tf_op jit(solution)/shard_map/scatter-add | solution.py:46
  667.0 84.7 %all-reduce.18.cloned.1.call-done = f32[512,256]{1,0:T(8,128)} async-done(((f32[512,256]{1,0:T(8,128)}), f32[512,256]{1,0:T(8,128)}) %all-reduce.18.cloned.1.call-update) | async-done | bytes 524304 | tf_op jit(solution)/shard_map/psum | solution.py:56
  754.6 16.1 %gather_fusion.5 = f32[4096,256]{1,0:T(8,128)} fusion(f32[512,256]{1,0:T(8,128)S(1)} %multiply_add_fusion.3, s32[4096]{0:T(1024)S(1)} %broadcast_clamp_fusion), kind=kCustom, calls=%fused_computation.5 | custom fusion | bytes 8404992 | tf_op jit(solution)/shard_map/gather | solution.py:45
  773.6 26.1 %scatter_custom_fusion.5 = f32[512,256]{1,0:T(8,128)} fusion(s32[4096]{0:T(1024)S(1)} %bitcast.61, f32[4096]{0:T(1024)S(1)} %fusion.56, f32[]{:T(128)} %constant.11.clone.1, bf16[4096,256]{1,0:T(8,128)(2,1)S(1)} %copy-done.1, pred[4096]{0:T(1024)(128)(4,1)S(1)} %compare_and_fusion), kind=kCustom, calls=%fused_computation.45 | custom fusion | flops 4194304 | bytes 2641924 | tf_op jit(solution)/shard_map/scatter-add | solution.py:46
  800.0 84.5 %all-reduce.20.cloned.1.call-done = f32[512,256]{1,0:T(8,128)} async-done(((f32[512,256]{1,0:T(8,128)}), f32[512,256]{1,0:T(8,128)}) %all-reduce.20.cloned.1.call-update) | async-done | bytes 524304 | tf_op jit(solution)/shard_map/psum | solution.py:56
  887.6 16.1 %gather_fusion.6 = f32[4096,256]{1,0:T(8,128)} fusion(f32[512,256]{1,0:T(8,128)S(1)} %multiply_add_fusion.2, s32[4096]{0:T(1024)S(1)} %broadcast_clamp_fusion), kind=kCustom, calls=%fused_computation.6 | custom fusion | bytes 8404992 | tf_op jit(solution)/shard_map/gather | solution.py:45
  907.2 26.5 %scatter_custom_fusion.6 = f32[512,256]{1,0:T(8,128)} fusion(s32[4096]{0:T(1024)S(1)} %bitcast.62, f32[4096]{0:T(1024)S(1)} %fusion.55, f32[]{:T(128)} %constant.11.clone.1, bf16[4096,256]{1,0:T(8,128)(2,1)} %copy-done, pred[4096]{0:T(1024)(128)(4,1)S(1)} %compare_and_fusion), kind=kCustom, calls=%fused_computation.47 | custom fusion | flops 4194304 | bytes 2641924 | tf_op jit(solution)/shard_map/scatter-add | solution.py:46
  933.8 84.7 %all-reduce.22.cloned.1.call-done = f32[512,256]{1,0:T(8,128)} async-done(((f32[512,256]{1,0:T(8,128)}), f32[512,256]{1,0:T(8,128)}) %all-reduce.22.cloned.1.call-update) | async-done | bytes 524304 | tf_op jit(solution)/shard_map/psum | solution.py:56
  1040.2 26.5 %scatter_custom_fusion.7 = f32[512,256]{1,0:T(8,128)} fusion(s32[4096]{0:T(1024)S(1)} %bitcast.63, f32[4096]{0:T(1024)S(1)} %fusion.54, f32[]{:T(128)} %constant.11.clone.1, bf16[4096,256]{1,0:T(8,128)(2,1)} %copy-done, pred[4096]{0:T(1024)(128)(4,1)S(1)} %compare_and_fusion), kind=kCustom, calls=%fused_computation.49 | custom fusion | flops 4194304 | bytes 2641924 | tf_op jit(solution)/shard_map/scatter-add | solution.py:46
  1067.0 84.5 %all-reduce.24.cloned.1.call-done = f32[512,256]{1,0:T(8,128)} async-done(((f32[512,256]{1,0:T(8,128)}), f32[512,256]{1,0:T(8,128)}) %all-reduce.24.cloned.1.call-update) | async-done | bytes 524304 | tf_op jit(solution)/shard_map/psum | solution.py:56
  1173.2 26.5 %scatter_custom_fusion.8 = f32[512,256]{1,0:T(8,128)} fusion(s32[4096]{0:T(1024)S(1)} %bitcast.64, f32[4096]{0:T(1024)S(1)} %fusion.53, f32[]{:T(128)} %constant.11.clone.1, bf16[4096,256]{1,0:T(8,128)(2,1)} %copy-done, pred[4096]{0:T(1024)(128)(4,1)S(1)} %compare_and_fusion), kind=kCustom, calls=%fused_computation.51 | custom fusion | flops 4194304 | bytes 2641924 | tf_op jit(solution)/shard_map/scatter-add | solution.py:46
  1200.1 84.5 %all-reduce.26.cloned.1.call-done = f32[512,256]{1,0:T(8,128)} async-done(((f32[512,256]{1,0:T(8,128)}), f32[512,256]{1,0:T(8,128)}) %all-reduce.26.cloned.1.call-update) | async-done | bytes 524304 | tf_op jit(solution)/shard_map/psum | solution.py:56
  (120 shorter events, 173.2 us)
Async XLA Ops:
  8.0 37.1 %all-gather.3.cloned.1.call-start = ((), (), s32[]{:S(2)}) async-start(), calls=%async_computation.9 | async-start | bytes 4718592 | tf_op jit(solution)/shard_map/all_gather | solution.py:30
  8.7 256.5 %all-reduce.12.cloned.1.call-start = ((), (), s32[]{:S(2)}) async-start(), calls=%async_computation.1 | async-start | bytes 524288 | tf_op jit(solution)/shard_map/psum | solution.py:33
  45.1 15.8 %copy-start.8 = (s32[1,1,4096]{2,1,0:T(1,128)S(1)}, s32[1,1,4096]{2,1,0:T(1,128)}, u32[]{:S(2)}) copy-start(s32[1,1,4096]{2,1,0:T(1,128)} %param.7) | copy-start | bytes 49156
  60.8 312.1 %copy-start = (bf16[4096,256]{1,0:T(8,128)(2,1)}, bf16[4096,256]{1,0:T(8,128)(2,1)S(1)}, u32[]{:S(2)}) copy-start(bf16[4096,256]{1,0:T(8,128)(2,1)S(1)} %gather_fusion) | copy-start | bytes 6291460
  86.3 14.1 %collective-permute-start = (f32[512,256]{1,0:T(8,128)S(1)}, f32[512,256]{1,0:T(8,128)S(1)}, u32[]{:S(2)}, u32[]{:S(2)}) collective-permute-start(f32[512,256]{1,0:T(8,128)S(1)} %scatter_custom_fusion), channel_id=1, source_target_pairs={{0,8},{8,0},{16,24},{24,16},{32,40},{40,32},{48,56},{56,48},{64,72... | collective-permute-start | bytes 1572872 | tf_op jit(solution)/shard_map/ppermute | solution.py:53
  100.5 14.8 %collective-permute-start.1 = (f32[512,256]{1,0:T(8,128)S(1)}, f32[512,256]{1,0:T(8,128)S(1)}, u32[]{:S(2)}, u32[]{:S(2)}) collective-permute-start(f32[512,256]{1,0:T(8,128)S(1)} %add.301), channel_id=1, source_target_pairs={{0,16},{8,24},{16,0},{24,8},{32,48},{40,56},{48,32},{56,40},{64,80... | collective-permute-start | bytes 1572872 | tf_op jit(solution)/shard_map/ppermute | solution.py:53
  115.4 12.4 collective-permute-start.2
  119.2 231.8 %all-reduce.10.cloned.1.call-start = ((), (), s32[]{:S(2)}) async-start(), calls=%async_computation | async-start | bytes 1048576 | tf_op jit(solution)/shard_map/psum | solution.py:56
  127.9 13.6 %collective-permute-start.3 = (f32[512,256]{1,0:T(8,128)S(1)}, f32[512,256]{1,0:T(8,128)S(1)}, u32[]{:S(2)}, u32[]{:S(2)}) collective-permute-start(f32[512,256]{1,0:T(8,128)S(1)} %add.303), channel_id=1, source_target_pairs={{0,64},{8,72},{16,80},{24,88},{32,96},{40,104},{48,112},{56,120},{... | collective-permute-start | bytes 1572872 | tf_op jit(solution)/shard_map/ppermute | solution.py:53
  157.7 3.0 copy-start.7
  186.8 297.0 %all-reduce.14.cloned.1.call-start = ((), (), s32[]{:S(2)}) async-start(), calls=%async_computation.2 | async-start | bytes 1048576 | tf_op jit(solution)/shard_map/psum | solution.py:56
  352.8 0.8 copy-start.3
  369.9 113.9 %copy-start.2 = (f32[256,256]{1,0:T(8,128)S(1)}, f32[256,256]{1,0:T(8,128)}, u32[]{:S(2)}) copy-start(f32[256,256]{1,0:T(8,128)} %all-reduce.12.cloned.1.call-done) | copy-start | bytes 786436
  399.1 219.6 %all-reduce.16.cloned.1.call-start = ((), (), s32[]{:S(2)}) async-start(), calls=%async_computation.3 | async-start | bytes 1048576 | tf_op jit(solution)/shard_map/psum | solution.py:56
  533.9 217.8 %all-reduce.18.cloned.1.call-start = ((), (), s32[]{:S(2)}) async-start(), calls=%async_computation.4 | async-start | bytes 1048576 | tf_op jit(solution)/shard_map/psum | solution.py:56
  620.6 1.0 copy-start.5
  621.7 16.1 %copy-start.1 = (bf16[4096,256]{1,0:T(8,128)(2,1)S(1)}, bf16[4096,256]{1,0:T(8,128)(2,1)}, u32[]{:S(2)}) copy-start(bf16[4096,256]{1,0:T(8,128)(2,1)} %copy-done) | copy-start | bytes 6291460
  637.7 115.6 %copy-start.6 = (f32[512,256]{1,0:T(8,128)S(1)}, f32[512,256]{1,0:T(8,128)}, u32[]{:S(2)}) copy-start(f32[512,256]{1,0:T(8,128)} %copy-done.5) | copy-start | bytes 1572868
  666.9 217.6 %all-reduce.20.cloned.1.call-start = ((), (), s32[]{:S(2)}) async-start(), calls=%async_computation.5 | async-start | bytes 1048576 | tf_op jit(solution)/shard_map/psum | solution.py:56
  753.6 0.8 copy-start.4
  799.7 218.8 %all-reduce.22.cloned.1.call-start = ((), (), s32[]{:S(2)}) async-start(), calls=%async_computation.6 | async-start | bytes 1048576 | tf_op jit(solution)/shard_map/psum | solution.py:56
  933.7 217.8 %all-reduce.24.cloned.1.call-start = ((), (), s32[]{:S(2)}) async-start(), calls=%async_computation.7 | async-start | bytes 1048576 | tf_op jit(solution)/shard_map/psum | solution.py:56
  1066.8 217.8 %all-reduce.26.cloned.1.call-start = ((), (), s32[]{:S(2)}) async-start(), calls=%async_computation.8 | async-start | bytes 1048576 | tf_op jit(solution)/shard_map/psum | solution.py:56
Sparse Core Ops, SparseCore 0:
  10.5 34.5 all-gather.2
Sparse Core Ops, SparseCore 1:
  119.3 145.9 all-reduce.11
  268.4 82.6 all-reduce.9
  399.1 84.6 all-reduce.13
  534.0 84.6 all-reduce.15
  667.0 84.6 all-reduce.17
  799.8 84.6 all-reduce.19
  933.8 84.7 all-reduce.21
  1066.8 84.7 all-reduce.23
  1199.8 84.6 all-reduce.25
